TPU v7x, 32 devices: a whole 2x2x4 slice. The times are simulated.
32 devices in a mesh: lon: 8 (over y, x, core), lat: 4 (over z).
Axes of the slice: x: 2, y: 2, z: 4, core: 2. Of those that a mesh axis runs over, the one named last changes fastest.
Arguments:
- latent: bfloat16 [4, 64, 128, 320], P(None, 'lat', 'lon'), may hold values from -28 to 28, as said below
- norm1_gain: float32 [320], replicated, may hold values from 0.1 to 1.9
- norm1_shift: float32 [320], replicated, may hold values from -3 to 3
- conv1_weight: bfloat16 [3, 3, 320, 320], replicated, may hold values from -0.109375 to 0.109375
- conv1_bias: float32 [320], replicated, may hold values from -3 to 3
- emb_shift: float32 [4, 320], replicated, may hold values from -4 to 4
- norm2_gain: float32 [320], replicated, may hold values from 0.1 to 1.9
- norm2_shift: float32 [320], replicated, may hold values from -3 to 3
- conv2_weight: bfloat16 [3, 3, 320, 320], replicated, may hold values from -0.109375 to 0.109375
- conv2_bias: float32 [320], replicated, may hold values from -3 to 3
Outputs:
- block_out: bfloat16 [4, 64, 128, 320], P(None, 'lat', 'lon')
Inputs may be any that keep to these rules, and one draw needn't show every extreme that they name: `latent`: Real-valued activations.
All inputs are finite; a program needn't handle non-finite values.
Results may differ from a plain program's by a relative error of at most 0.007.
Values may be sent and summed in bfloat16 or wider, within the bound.
No kernel may reach another device: no remote copies, remote signals or barrier semaphores. Data moves between devices by JAX's collectives and lax.ppermute only.
A program may use at most 64 MiB of HBM per device.

v0:
```python
import jax
import jax.numpy as jnp
from jax import lax
from jax.sharding import PartitionSpec as P

GROUPS = 32


def padded_2(array, sides, width, wrap):
    for axis, dim in sides:
        devices, length = (lax.axis_size(axis), array.shape[dim])
        up = [(i, (i + 1) % devices) for i in range(devices if wrap else devices - 1)]
        down = [(j, i) for i, j in up]
        last = lax.slice_in_dim(array, length - width, length, axis=dim)
        leading = lax.slice_in_dim(array, 0, width, axis=dim)
        before = lax.ppermute(last, axis, up)
        after = lax.ppermute(leading, axis, down)
        array = jnp.concatenate([before, array, after], axis=dim)
    return array


def from_behind(array, axis, by):
    devices = lax.axis_size(axis)
    return lax.ppermute(array, axis, [(i, (i + by) % devices) for i in range(devices)])


def group_stats(field, cell_count):
    frame_count = field.shape[0]
    grouped = field.reshape(frame_count, -1, GROUPS, field.shape[3] // GROUPS)
    summed, squares = lax.psum(
        (jnp.sum(grouped, axis=(1, 3)), jnp.sum(grouped * grouped, axis=(1, 3))), ("lon", "lat")
    )
    average = summed / cell_count
    variance = squares / cell_count - average * average
    return (average, lax.rsqrt(variance + 1e-05))


def activate(field, average, inverse, norm_gain, norm_shift):
    per_group = field.shape[3] // GROUPS
    per_mean = jnp.repeat(average, per_group, axis=1)[:, None, None, :]
    per_inverse = jnp.repeat(inverse, per_group, axis=1)[:, None, None, :]
    normed = (field - per_mean) * per_inverse * norm_gain + norm_shift
    return jax.nn.silu(normed).astype(jnp.bfloat16)


def sphere_pad(field):
    side_padded = padded_2(field, (("lon", 2),), 1, True)
    both_padded = padded_2(side_padded, (("lat", 1),), 1, False)
    north_row, south_row = from_behind(
        (side_padded[:, 0], side_padded[:, -1]), "lon", lax.axis_size("lon") // 2
    )
    lat_index = lax.axis_index("lat")
    first_row = jnp.where(lat_index == 0, north_row, both_padded[:, 0])
    final_row = jnp.where(lat_index == lax.axis_size("lat") - 1, south_row, both_padded[:, -1])
    return jnp.concatenate([first_row[:, None], both_padded[:, 1:-1], final_row[:, None]], axis=1)


def padded_input(source, cell_count, norm_gain, norm_shift):
    source_f = source.astype(jnp.float32)
    average, inverse = group_stats(source_f, cell_count)
    return sphere_pad(activate(source_f, average, inverse, norm_gain, norm_shift))


def convolve(padded, weight):
    return lax.conv_general_dilated(
        padded,
        weight,
        (1, 1),
        "VALID",
        dimension_numbers=("NHWC", "HWIO", "NHWC"),
        preferred_element_type=jnp.float32,
    )


def on_device(
    latent,
    norm1_gain,
    norm1_shift,
    conv1_weight,
    conv1_bias,
    emb_shift,
    norm2_gain,
    norm2_shift,
    conv2_weight,
    conv2_bias,
):
    per_group = latent.shape[3] // GROUPS
    cell_count = (
        latent.shape[1] * latent.shape[2] * lax.axis_size("lat") * lax.axis_size("lon") * per_group
    )
    first_padded = padded_input(latent, cell_count, norm1_gain, norm1_shift)
    hidden = convolve(first_padded, conv1_weight) + conv1_bias + emb_shift[:, None, None, :]
    hidden = hidden.astype(jnp.bfloat16)
    second_padded = padded_input(hidden, cell_count, norm2_gain, norm2_shift)
    branch = convolve(second_padded, conv2_weight) + conv2_bias
    return (latent.astype(jnp.float32) + branch).astype(jnp.bfloat16)


def solution(mesh):
    placed = (P(None, "lat", "lon", None), P(), P(), P(), P(), P(), P(), P(), P(), P())
    return jax.shard_map(
        on_device,
        mesh=mesh,
        in_specs=placed,
        out_specs=P(None, "lat", "lon", None),
        check_vma=False,
    )
```

profile of v0, /device:TPU:0, one launch (start us, length us, event | category | flops | bytes accessed | tf_op | source)
XLA Modules:
  0.0 154.9 jit_solution(12832509377845679093)
XLA Ops:
  0.0 2.1 %convert_reduce_fusion = (f32[4,320]{1,0:T(4,128)S(1)}, f32[4,320]{1,0:T(4,128)S(1)}) fusion(bf16[4,16,16,320]{3,2,1,0:T(8,128)(2,1)} %param.10), kind=kLoop, calls=%fused_computation.6 | loop fusion | flops 1308160 | bytes 665600 | tf_op jit(solution)/shard_map/reduce_sum | solution.py:31
  2.1 0.1 reduce_sum.47
  2.2 0.1 reduce_sum.53
  2.4 0.1 reduce_sum.51
  2.5 0.1 reduce_sum.54
  2.6 42.0 %all-reduce.1 = (f32[4,32]{1,0:T(4,128)S(1)}, f32[4,32]{1,0:T(4,128)S(1)}) all-reduce(f32[4,32]{1,0:T(4,128)S(1)} %reduce_sum.54, f32[4,32]{1,0:T(4,128)S(1)} %reduce_sum.51), channel_id=1, replica_groups=mesh['lon'=8,'lat'=4] {'lon','lat'}, use_global_device_ids=true, to_apply=%region_5.6 | all-reduce | flops 256 | bytes 2048 | tf_op jit(solution)/shard_map/psum | solution.py:30
  44.6 0.1 sub.26
  44.8 0.1 mul.59
  45.0 2.4 %fusion.18 = bf16[4,16,16,320]{3,0,2,1:T(4,128)(2,1)S(1)} fusion(f32[320]{0:T(512)} %param.12, f32[320]{0:T(512)} %param.11, f32[4,320]{1,0:T(4,128)S(1)} %mul.59, f32[4,320]{1,0:T(4,128)S(1)} %sub.26, bf16[4,16,16,320]{3,2,1,0:T(8,128)(2,1)} %param.10), kind=kLoop, calls=%fused_computation.32 | loop fusion | flops 3276800 | bytes 1323520 | tf_op jit(solution)/shard_map/convert_element_type | solution.py:43
  47.5 2.6 %collective-permute-start.1 = (bf16[4,16,1,320]{3,0,2,1:T(4,128)(2,1)S(1)}, bf16[4,16,1,320]{3,0,2,1:T(4,128)(2,1)S(1)}, u32[]{:S(2)}, u32[]{:S(2)}) collective-permute-start(bf16[4,16,1,320]{3,0,2,1:T(4,128)(2,1)S(1)} %get-tuple-element.18), channel_id=1, source_target_pairs={{4,0},{8,4},{12,8},{16,12},{20,16},{24,20},{28,24},{0,28},{5,1},{9... | collective-permute-start | bytes 122888 | tf_op jit(solution)/shard_map/ppermute | solution.py:17
  50.1 1.8 %collective-permute-done = bf16[4,16,1,320]{3,0,2,1:T(4,128)(2,1)S(1)} collective-permute-done((bf16[4,16,1,320]{3,0,2,1:T(4,128)(2,1)S(1)}, bf16[4,16,1,320]{3,0,2,1:T(4,128)(2,1)S(1)}, u32[]{:S(2)}, u32[]{:S(2)}) %collective-permute-start) | collective-permute-done | bytes 40992 | tf_op jit(solution)/shard_map/ppermute | solution.py:16
  51.9 0.1 pad_maximum_fusion.5
  52.0 2.3 %collective-permute-start.4 = (bf16[4,18,320]{2,0,1:T(4,128)(2,1)S(1)}, bf16[4,18,320]{2,0,1:T(4,128)(2,1)S(1)}, u32[]{:S(2)}, u32[]{:S(2)}) collective-permute-start(bf16[4,18,320]{2,0,1:T(4,128)(2,1)S(1)} %bitcast.78), channel_id=1, source_target_pairs={{0,16},{4,20},{8,24},{12,28},{16,0},{20,4},{24,8},{28,12},{1,17},{... | collective-permute-start | bytes 138248 | tf_op jit(solution)/shard_map/ppermute | solution.py:24
  54.3 1.3 collective-permute-start.5
  55.6 4.7 %collective-permute-start.3 = (bf16[4,1,18,320]{3,0,2,1:T(4,128)(2,1)S(1)}, bf16[4,1,18,320]{3,0,2,1:T(4,128)(2,1)S(1)}, u32[]{:S(2)}, u32[]{:S(2)}) collective-permute-start(bf16[4,1,18,320]{3,0,2,1:T(4,128)(2,1)S(1)} %get-tuple-element.14), channel_id=1, source_target_pairs={{0,1},{1,2},{2,3},{4,5},{5,6},{6,7},{8,9},{9,10},{10,11},{12,13},{... | collective-permute-start | bytes 138248 | tf_op jit(solution)/shard_map/ppermute | solution.py:16
  60.4 0.1 collective-permute-start.2
  60.5 4.1 %collective-permute-done.2 = bf16[4,18,320]{2,0,1:T(4,128)(2,1)S(1)} collective-permute-done((bf16[4,18,320]{2,0,1:T(4,128)(2,1)S(1)}, bf16[4,18,320]{2,0,1:T(4,128)(2,1)S(1)}, u32[]{:S(2)}, u32[]{:S(2)}) %collective-permute-start.2) | collective-permute-done | bytes 46112 | tf_op jit(solution)/shard_map/ppermute | solution.py:24
  64.6 0.9 maximum_bitcast_fusion.1
  65.6 0.5 pad
  66.1 0.3 slice.44
  66.4 1.0 fusion.5
  67.5 0.2 broadcast.25
  67.6 0.5 copy-done.7
  68.1 7.1 %fusion.30 = (f32[16,32,3,320]{3,1,2,0:T(8,128)S(1)}, f32[16,32,3,320]{3,1,2,0:T(8,128)}) fusion(f32[16,32,3,320]{3,0,2,1:T(8,128)S(1)} %bitcast.75, f32[320]{0:T(512)S(1)} %copy-done.7, bf16[3,3,320,320]{3,2,1,0:T(8,128)(2,1)S(1)} %copy-done, bf16[18,4,8,5,320]{4,1,3,2,0:T(4,128)(2,1)S(1)} %fusion.5, pred[32,3]{0,1:T(4,128)(4,1)S(1)} %copy-done.9), kind=kOutput, calls=%fused_computation.59 | convolution fusion | flops 2834104320 | bytes 9586016 | tf_op jit(solution)/shard_map/conv_general_dilated | solution.py:65
  75.2 1.4 copy.121
  76.6 0.1 slice_reduce_fusion
  76.7 0.1 reduce_sum.74
  76.8 0.1 reduce_sum.75
  76.9 3.0 %copy.119 = f32[16,32,3,320]{3,0,2,1:T(8,128)S(1)} copy(f32[16,32,3,320]{3,1,2,0:T(8,128)} %get-tuple-element.24) | data formatting | bytes 3932160 | tf_op jit(solution)/shard_map/convert_element_type | solution.py:59
  79.9 0.1 slice_reduce_fusion.1
  80.0 0.1 reduce_sum.59
  80.2 0.1 reduce_sum.72
  80.2 39.4 %all-reduce = (f32[4,32]{1,0:T(4,128)S(1)}, f32[4,32]{1,0:T(4,128)S(1)}) all-reduce(f32[4,32]{1,0:T(4,128)S(1)} %reduce_sum.75, f32[4,32]{1,0:T(4,128)S(1)} %reduce_sum.72), channel_id=1, replica_groups=mesh['lon'=8,'lat'=4] {'lon','lat'}, use_global_device_ids=true, to_apply=%region_11.12 | all-reduce | flops 256 | bytes 2048 | tf_op jit(solution)/shard_map/psum | solution.py:30
  119.7 0.1 sub.30
  119.9 0.1 mul.67
  120.1 0.2 broadcast.27
  120.3 0.2 broadcast.26
  120.4 1.3 copy-done.1
  121.7 1.8 %multiply_convert_fusion = bf16[16,32,3,320]{3,1,2,0:T(8,128)(2,1)S(1)} fusion(f32[16,32,3,320]{3,0,2,1:T(8,128)S(1)} %bitcast.65, f32[16,32,3,320]{3,1,2,0:T(8,128)S(1)} %copy-done.1, f32[16,32,3,320]{3,0,2,1:T(8,128)S(1)} %bitcast.66, f32[320]{0:T(512)S(1)} %copy-done.4, f32[320]{0:T(512)S(1)} %copy-done.5), kind=kLoop, calls=%fused_computation.14 | loop fusion | flops 4423680 | bytes 6883840 | tf_op jit(solution)/shard_map/convert_element_type | solution.py:43
  123.5 0.4 copy.123
  123.9 0.1 slice_bitcast_fusion
  124.1 2.6 %collective-permute-start.7 = (bf16[4,16,1,320]{3,1,2,0:T(8,128)(2,1)S(1)}, bf16[4,16,1,320]{3,1,2,0:T(8,128)(2,1)S(1)}, u32[]{:S(2)}, u32[]{:S(2)}) collective-permute-start(bf16[4,16,1,320]{3,1,2,0:T(8,128)(2,1)S(1)} %get-tuple-element.16), channel_id=1, source_target_pairs={{4,0},{8,4},{12,8},{16,12},{20,16},{24,20},{28,24},{0,28},{5,1},{9... | collective-permute-start | bytes 122888 | tf_op jit(solution)/shard_map/ppermute | solution.py:17
  126.7 1.8 %collective-permute-done.6 = bf16[4,16,1,320]{3,1,2,0:T(8,128)(2,1)S(1)} collective-permute-done((bf16[4,16,1,320]{3,1,2,0:T(8,128)(2,1)S(1)}, bf16[4,16,1,320]{3,1,2,0:T(8,128)(2,1)S(1)}, u32[]{:S(2)}, u32[]{:S(2)}) %collective-permute-start.6) | collective-permute-done | bytes 40992 | tf_op jit(solution)/shard_map/ppermute | solution.py:16
  128.5 0.2 pad_maximum_fusion.2
  128.7 2.3 %collective-permute-start.10 = (bf16[4,18,320]{2,0,1:T(4,128)(2,1)S(1)}, bf16[4,18,320]{2,0,1:T(4,128)(2,1)S(1)}, u32[]{:S(2)}, u32[]{:S(2)}) collective-permute-start(bf16[4,18,320]{2,0,1:T(4,128)(2,1)S(1)} %bitcast.77), channel_id=1, source_target_pairs={{0,16},{4,20},{8,24},{12,28},{16,0},{20,4},{24,8},{28,12},{1,17},{... | collective-permute-start | bytes 138248 | tf_op jit(solution)/shard_map/ppermute | solution.py:24
  131.1 1.3 collective-permute-start.11
  132.4 4.6 %collective-permute-start.9 = (bf16[4,1,18,320]{3,1,2,0:T(2,128)(2,1)S(1)}, bf16[4,1,18,320]{3,1,2,0:T(2,128)(2,1)S(1)}, u32[]{:S(2)}, u32[]{:S(2)}) collective-permute-start(bf16[4,1,18,320]{3,1,2,0:T(2,128)(2,1)S(1)} %get-tuple-element.12), channel_id=1, source_target_pairs={{0,1},{1,2},{2,3},{4,5},{5,6},{6,7},{8,9},{9,10},{10,11},{12,13},{... | collective-permute-start | bytes 138248 | tf_op jit(solution)/shard_map/ppermute | solution.py:16
  137.0 0.1 collective-permute-start.8
  137.1 0.6 collective-permute-done.11
  137.8 0.1 copy.129
  137.9 3.3 %collective-permute-done.8 = bf16[4,18,320]{2,0,1:T(4,128)(2,1)S(1)} collective-permute-done((bf16[4,18,320]{2,0,1:T(4,128)(2,1)S(1)}, bf16[4,18,320]{2,0,1:T(4,128)(2,1)S(1)}, u32[]{:S(2)}, u32[]{:S(2)}) %collective-permute-start.8) | collective-permute-done | bytes 46112 | tf_op jit(solution)/shard_map/ppermute | solution.py:24
  141.2 0.1 copy.128
  141.3 0.9 maximum_bitcast_fusion
  142.2 0.4 copy.136
  142.6 0.5 pad.2.clone
  143.1 0.3 slice.50
  143.4 1.0 fusion.6
  144.5 0.5 copy-done.6
  145.0 5.0 %select_add_fusion = f32[16,32,3,320]{3,1,2,0:T(8,128)S(1)} fusion(bf16[3,3,320,320]{3,2,1,0:T(8,128)(2,1)S(1)} %copy-done.6, bf16[18,4,8,5,320]{4,1,3,2,0:T(4,128)(2,1)S(1)} %fusion.6, f32[320]{0:T(512)S(1)} %copy-done.8, pred[32,3]{0,1:T(4,128)(4,1)S(1)} %copy-done.9), kind=kOutput, calls=%fused_computation.13 | convolution fusion | flops 2832138240 | bytes 5653856 | tf_op jit(solution)/shard_map/conv_general_dilated | solution.py:65
  150.0 1.4 copy.132
  151.4 0.1 slice.51
  151.5 1.0 copy-done.2
  152.5 1.4 fusion.17
  154.0 1.0 copy.134
  (39 shorter events, 0.8 us)
Async XLA Ops:
  0.0 67.6 %copy-start = (bf16[3,3,320,320]{3,2,1,0:T(8,128)(2,1)S(1)}, bf16[3,3,320,320]{3,2,1,0:T(8,128)(2,1)}, u32[]{:S(2)}) copy-start(bf16[3,3,320,320]{3,2,1,0:T(8,128)(2,1)} %param.13) | copy-start | bytes 5529604
  47.4 4.5 %collective-permute-start = (bf16[4,16,1,320]{3,0,2,1:T(4,128)(2,1)S(1)}, bf16[4,16,1,320]{3,0,2,1:T(4,128)(2,1)S(1)}, u32[]{:S(2)}, u32[]{:S(2)}) collective-permute-start(bf16[4,16,1,320]{3,0,2,1:T(4,128)(2,1)S(1)} %get-tuple-element.17), channel_id=1, source_target_pairs={{0,4},{4,8},{8,12},{12,16},{16,20},{20,24},{24,28},{28,0},{1,5},{5... | collective-permute-start | bytes 122888 | tf_op jit(solution)/shard_map/ppermute | solution.py:16
  47.5 4.4 %collective-permute-start.1 = (bf16[4,16,1,320]{3,0,2,1:T(4,128)(2,1)S(1)}, bf16[4,16,1,320]{3,0,2,1:T(4,128)(2,1)S(1)}, u32[]{:S(2)}, u32[]{:S(2)}) collective-permute-start(bf16[4,16,1,320]{3,0,2,1:T(4,128)(2,1)S(1)} %get-tuple-element.18), channel_id=1, source_target_pairs={{4,0},{8,4},{12,8},{16,12},{20,16},{24,20},{28,24},{0,28},{5,1},{9... | collective-permute-start | bytes 122888 | tf_op jit(solution)/shard_map/ppermute | solution.py:17
  52.0 8.5 %collective-permute-start.4 = (bf16[4,18,320]{2,0,1:T(4,128)(2,1)S(1)}, bf16[4,18,320]{2,0,1:T(4,128)(2,1)S(1)}, u32[]{:S(2)}, u32[]{:S(2)}) collective-permute-start(bf16[4,18,320]{2,0,1:T(4,128)(2,1)S(1)} %bitcast.78), channel_id=1, source_target_pairs={{0,16},{4,20},{8,24},{12,28},{16,0},{20,4},{24,8},{28,12},{1,17},{... | collective-permute-start | bytes 138248 | tf_op jit(solution)/shard_map/ppermute | solution.py:24
  54.3 6.1 %collective-permute-start.5 = (bf16[4,1,18,320]{3,0,2,1:T(4,128)(2,1)S(1)}, bf16[4,1,18,320]{3,0,2,1:T(4,128)(2,1)S(1)}, u32[]{:S(2)}, u32[]{:S(2)}) collective-permute-start(bf16[4,1,18,320]{3,0,2,1:T(4,128)(2,1)S(1)} %get-tuple-element.13), channel_id=1, source_target_pairs={{1,0},{2,1},{3,2},{5,4},{6,5},{7,6},{9,8},{10,9},{11,10},{13,12},{... | collective-permute-start | bytes 138248 | tf_op jit(solution)/shard_map/ppermute | solution.py:17
  55.6 9.0 %collective-permute-start.3 = (bf16[4,1,18,320]{3,0,2,1:T(4,128)(2,1)S(1)}, bf16[4,1,18,320]{3,0,2,1:T(4,128)(2,1)S(1)}, u32[]{:S(2)}, u32[]{:S(2)}) collective-permute-start(bf16[4,1,18,320]{3,0,2,1:T(4,128)(2,1)S(1)} %get-tuple-element.14), channel_id=1, source_target_pairs={{0,1},{1,2},{2,3},{4,5},{5,6},{6,7},{8,9},{9,10},{10,11},{12,13},{... | collective-permute-start | bytes 138248 | tf_op jit(solution)/shard_map/ppermute | solution.py:16
  60.4 4.2 %collective-permute-start.2 = (bf16[4,18,320]{2,0,1:T(4,128)(2,1)S(1)}, bf16[4,18,320]{2,0,1:T(4,128)(2,1)S(1)}, u32[]{:S(2)}, u32[]{:S(2)}) collective-permute-start(bf16[4,18,320]{2,0,1:T(4,128)(2,1)S(1)} %bitcast.79), channel_id=1, source_target_pairs={{0,16},{4,20},{8,24},{12,28},{16,0},{20,4},{24,8},{28,12},{1,17},{... | collective-permute-start | bytes 138248 | tf_op jit(solution)/shard_map/ppermute | solution.py:24
  66.4 1.1 copy-start.3
  67.4 0.7 copy-start.7
  67.4 0.7 copy-start.9
  120.1 1.7 %copy-start.1 = (f32[16,32,3,320]{3,1,2,0:T(8,128)S(1)}, f32[16,32,3,320]{3,1,2,0:T(8,128)}, u32[]{:S(2)}) copy-start(f32[16,32,3,320]{3,1,2,0:T(8,128)} %get-tuple-element.24) | copy-start | bytes 5898244
  120.1 1.7 %copy-start.4 = (f32[320]{0:T(512)S(1)}, f32[320]{0:T(512)}, u32[]{:S(2)}) copy-start(f32[320]{0:T(512)} %param.17) | copy-start | bytes 3844
  120.1 1.7 %copy-start.5 = (f32[320]{0:T(512)S(1)}, f32[320]{0:T(512)}, u32[]{:S(2)}) copy-start(f32[320]{0:T(512)} %param.16) | copy-start | bytes 3844
  124.0 4.5 %collective-permute-start.6 = (bf16[4,16,1,320]{3,1,2,0:T(8,128)(2,1)S(1)}, bf16[4,16,1,320]{3,1,2,0:T(8,128)(2,1)S(1)}, u32[]{:S(2)}, u32[]{:S(2)}) collective-permute-start(bf16[4,16,1,320]{3,1,2,0:T(8,128)(2,1)S(1)} %get-tuple-element.15), channel_id=1, source_target_pairs={{0,4},{4,8},{8,12},{12,16},{16,20},{20,24},{24,28},{28,0},{1,5},{5... | collective-permute-start | bytes 122888 | tf_op jit(solution)/shard_map/ppermute | solution.py:16
  124.1 4.4 %collective-permute-start.7 = (bf16[4,16,1,320]{3,1,2,0:T(8,128)(2,1)S(1)}, bf16[4,16,1,320]{3,1,2,0:T(8,128)(2,1)S(1)}, u32[]{:S(2)}, u32[]{:S(2)}) collective-permute-start(bf16[4,16,1,320]{3,1,2,0:T(8,128)(2,1)S(1)} %get-tuple-element.16), channel_id=1, source_target_pairs={{4,0},{8,4},{12,8},{16,12},{20,16},{24,20},{28,24},{0,28},{5,1},{9... | collective-permute-start | bytes 122888 | tf_op jit(solution)/shard_map/ppermute | solution.py:17
  128.7 8.3 %collective-permute-start.10 = (bf16[4,18,320]{2,0,1:T(4,128)(2,1)S(1)}, bf16[4,18,320]{2,0,1:T(4,128)(2,1)S(1)}, u32[]{:S(2)}, u32[]{:S(2)}) collective-permute-start(bf16[4,18,320]{2,0,1:T(4,128)(2,1)S(1)} %bitcast.77), channel_id=1, source_target_pairs={{0,16},{4,20},{8,24},{12,28},{16,0},{20,4},{24,8},{28,12},{1,17},{... | collective-permute-start | bytes 138248 | tf_op jit(solution)/shard_map/ppermute | solution.py:24
  131.1 6.6 %collective-permute-start.11 = (bf16[4,1,18,320]{3,1,2,0:T(2,128)(2,1)S(1)}, bf16[4,1,18,320]{3,1,2,0:T(2,128)(2,1)S(1)}, u32[]{:S(2)}, u32[]{:S(2)}) collective-permute-start(bf16[4,1,18,320]{3,1,2,0:T(2,128)(2,1)S(1)} %get-tuple-element.11), channel_id=1, source_target_pairs={{1,0},{2,1},{3,2},{5,4},{6,5},{7,6},{9,8},{10,9},{11,10},{13,12},{... | collective-permute-start | bytes 138248 | tf_op jit(solution)/shard_map/ppermute | solution.py:17
  132.4 8.8 %collective-permute-start.9 = (bf16[4,1,18,320]{3,1,2,0:T(2,128)(2,1)S(1)}, bf16[4,1,18,320]{3,1,2,0:T(2,128)(2,1)S(1)}, u32[]{:S(2)}, u32[]{:S(2)}) collective-permute-start(bf16[4,1,18,320]{3,1,2,0:T(2,128)(2,1)S(1)} %get-tuple-element.12), channel_id=1, source_target_pairs={{0,1},{1,2},{2,3},{4,5},{5,6},{6,7},{8,9},{9,10},{10,11},{12,13},{... | collective-permute-start | bytes 138248 | tf_op jit(solution)/shard_map/ppermute | solution.py:16
  137.0 4.2 %collective-permute-start.8 = (bf16[4,18,320]{2,0,1:T(4,128)(2,1)S(1)}, bf16[4,18,320]{2,0,1:T(4,128)(2,1)S(1)}, u32[]{:S(2)}, u32[]{:S(2)}) collective-permute-start(bf16[4,18,320]{2,0,1:T(4,128)(2,1)S(1)} %bitcast.76), channel_id=1, source_target_pairs={{0,16},{4,20},{8,24},{12,28},{16,0},{20,4},{24,8},{28,12},{1,17},{... | collective-permute-start | bytes 138248 | tf_op jit(solution)/shard_map/ppermute | solution.py:24
  143.4 1.6 %copy-start.6 = (bf16[3,3,320,320]{3,2,1,0:T(8,128)(2,1)S(1)}, bf16[3,3,320,320]{3,2,1,0:T(8,128)(2,1)}, u32[]{:S(2)}) copy-start(bf16[3,3,320,320]{3,2,1,0:T(8,128)(2,1)} %param.18) | copy-start | bytes 5529604
  143.4 1.6 %copy-start.8 = (f32[320]{0:T(512)S(1)}, f32[320]{0:T(512)}, u32[]{:S(2)}) copy-start(f32[320]{0:T(512)} %param.19) | copy-start | bytes 3844
  151.4 1.1 copy-start.2
where the time goes:
time: 156 us; the launch traced here: 155 us
  blocking collectives  81.4 us (52%)
  starting transfers between devices  22.1 us (14%)
  local copies, waits for them, and re-layouts  14.6 us (9%)
  other arithmetic  12.7 us (8%)
  matrix products  12.1 us (8%)
  waiting for transfers between devices  11.6 us (7%)
    psum x2, blocking collectives, group_stats(): lax.psum((jnp.sum(grouped, axis=(1, 3)), jnp.sum(grouped * grouped, axis=...  81.4 us
    conv_general_dilated x2, matrix products, convolve(): lax.conv_general_dilated(padded, weight, (1, 1), 'VALID', dimension_numbe...  12.1 us
    ppermute x4, starting transfers between devices, padded_2(): before = lax.ppermute(last, axis, up)  9.4 us
    ppermute x4, starting transfers between devices, padded_2(): after = lax.ppermute(leading, axis, down)  7.82 us
    ppermute x4, waiting for transfers between devices, from_behind(): lax.ppermute(array, axis, [(i, (i + by) % devices) for i in range(devices)])  7.42 us
    ppermute x4, starting transfers between devices, from_behind(): lax.ppermute(array, axis, [(i, (i + by) % devices) for i in range(devices)])  4.85 us
    convert_element_type x2, other arithmetic, activate(): return jax.nn.silu(normed).astype(jnp.bfloat16)  4.24 us
    unnamed x21, local copies, waits for them, and re-layouts  3.76 us
  transfers between devices with their start and end apart: 12, of which 5 were waited for; matrix products, arithmetic and copies ran while one was open for 0% of the time, Pallas kernels for 0%

commit v1 on v0

--- a/solution.py
+++ b/solution.py
@@ -27,8 +27,16 @@
 def group_stats(field, cell_count):
     frame_count = field.shape[0]
     grouped = field.reshape(frame_count, -1, GROUPS, field.shape[3] // GROUPS)
-    summed, squares = lax.psum(
-        (jnp.sum(grouped, axis=(1, 3)), jnp.sum(grouped * grouped, axis=(1, 3))), ("lon", "lat")
+
+    def step_on_the_pairs_all(local):
+        mesh_name = "lon"
+        comm_axis = "lat"
+        for p in (mesh_name, comm_axis):
+            local = lax.psum(local, p)
+        return local
+
+    summed, squares = step_on_the_pairs_all(
+        (jnp.sum(grouped, axis=(1, 3)), jnp.sum(grouped * grouped, axis=(1, 3)))
     )
     average = summed / cell_count
     variance = squares / cell_count - average * average

time: 156 us -> 120 us (0.77)
  blocking collectives: 81.4 us -> 48.4 us
  waiting for transfers between devices: 11.6 us -> 9.65 us
    psum x2 -> x4, blocking collectives: 81.4 us -> 48.4 us  [step_on_the_pairs_all(): local = lax.psum(local, p)]
where the time goes in v1:
time: 120 us; the launch traced here: 119 us
  blocking collectives  48.4 us (40%)
  starting transfers between devices  21.5 us (18%)
  local copies, waits for them, and re-layouts  14.6 us (12%)
  other arithmetic  12.7 us (11%)
  matrix products  12.1 us (10%)
  waiting for transfers between devices  9.65 us (8%)
    psum x4, blocking collectives, step_on_the_pairs_all(): local = lax.psum(local, p)  48.4 us
    conv_general_dilated x2, matrix products, convolve(): lax.conv_general_dilated(padded, weight, (1, 1), 'VALID', dimension_numbe...  12.1 us
    ppermute x4, starting transfers between devices, padded_2(): before = lax.ppermute(last, axis, up)  9.4 us
    ppermute x4, starting transfers between devices, padded_2(): after = lax.ppermute(leading, axis, down)  7.82 us
    ppermute x4, waiting for transfers between devices, from_behind(): lax.ppermute(array, axis, [(i, (i + by) % devices) for i in range(devices)])  5.93 us
    ppermute x4, starting transfers between devices, from_behind(): lax.ppermute(array, axis, [(i, (i + by) % devices) for i in range(devices)])  4.31 us
    convert_element_type x2, other arithmetic, activate(): return jax.nn.silu(normed).astype(jnp.bfloat16)  4.24 us
    unnamed x21, local copies, waits for them, and re-layouts  3.76 us
  transfers between devices with their start and end apart: 12, of which 5 were waited for; matrix products, arithmetic and copies ran while one was open for 0% of the time, Pallas kernels for 0%

profile of v1, /device:TPU:0, one launch (start us, length us, event | category | flops | bytes accessed | tf_op | source)
XLA Modules:
  0.0 119.4 jit_solution(3777234880564308092)
XLA Ops:
  0.0 2.1 %convert_reduce_fusion = (f32[4,320]{1,0:T(4,128)S(1)}, f32[4,320]{1,0:T(4,128)S(1)}) fusion(bf16[4,16,16,320]{3,2,1,0:T(8,128)(2,1)} %param.10), kind=kLoop, calls=%fused_computation.6 | loop fusion | flops 1308160 | bytes 665600 | tf_op jit(solution)/shard_map/reduce_sum | solution.py:39
  2.1 0.1 reduce_sum.47
  2.2 0.1 reduce_sum.53
  2.4 0.1 reduce_sum.51
  2.5 0.1 reduce_sum.54
  2.6 15.2 %all-reduce.1 = (f32[4,32]{1,0:T(4,128)S(1)}, f32[4,32]{1,0:T(4,128)S(1)}) all-reduce(f32[4,32]{1,0:T(4,128)S(1)} %reduce_sum.54, f32[4,32]{1,0:T(4,128)S(1)} %reduce_sum.51), channel_id=1, replica_groups=mesh['lon'=8,'lat'=4] {'lon'}, use_global_device_ids=true, to_apply=%region_6.7 | all-reduce | flops 256 | bytes 2048 | tf_op jit(solution)/shard_map/psum | solution.py:35
  17.7 11.9 %all-reduce.3 = (f32[4,32]{1,0:T(4,128)S(1)}, f32[4,32]{1,0:T(4,128)S(1)}) all-reduce(f32[4,32]{1,0:T(4,128)S(1)} %get-tuple-element.9, f32[4,32]{1,0:T(4,128)S(1)} %get-tuple-element.10), channel_id=1, replica_groups=mesh['lon'=8,'lat'=4] {'lat'}, use_global_device_ids=true, to_apply=%region_7.8 | all-reduce | flops 256 | bytes 2048 | tf_op jit(solution)/shard_map/psum | solution.py:35
  29.7 0.1 sub.26
  29.9 0.1 mul.59
  30.1 2.4 %fusion.18 = bf16[4,16,16,320]{3,0,2,1:T(4,128)(2,1)S(1)} fusion(f32[320]{0:T(512)} %param.12, f32[320]{0:T(512)} %param.11, f32[4,320]{1,0:T(4,128)S(1)} %mul.59, f32[4,320]{1,0:T(4,128)S(1)} %sub.26, bf16[4,16,16,320]{3,2,1,0:T(8,128)(2,1)} %param.10), kind=kLoop, calls=%fused_computation.32 | loop fusion | flops 3276800 | bytes 1323520 | tf_op jit(solution)/shard_map/convert_element_type | solution.py:51
  32.6 2.6 %collective-permute-start.1 = (bf16[4,16,1,320]{3,0,2,1:T(4,128)(2,1)S(1)}, bf16[4,16,1,320]{3,0,2,1:T(4,128)(2,1)S(1)}, u32[]{:S(2)}, u32[]{:S(2)}) collective-permute-start(bf16[4,16,1,320]{3,0,2,1:T(4,128)(2,1)S(1)} %get-tuple-element.22), channel_id=1, source_target_pairs={{4,0},{8,4},{12,8},{16,12},{20,16},{24,20},{28,24},{0,28},{5,1},{9... | collective-permute-start | bytes 122888 | tf_op jit(solution)/shard_map/ppermute | solution.py:17
  35.3 1.8 %collective-permute-done = bf16[4,16,1,320]{3,0,2,1:T(4,128)(2,1)S(1)} collective-permute-done((bf16[4,16,1,320]{3,0,2,1:T(4,128)(2,1)S(1)}, bf16[4,16,1,320]{3,0,2,1:T(4,128)(2,1)S(1)}, u32[]{:S(2)}, u32[]{:S(2)}) %collective-permute-start) | collective-permute-done | bytes 40992 | tf_op jit(solution)/shard_map/ppermute | solution.py:16
  37.0 0.1 pad_maximum_fusion.5
  37.1 0.6 collective-permute-start.4
  37.7 1.3 %collective-permute-start.5 = (bf16[4,1,18,320]{3,0,2,1:T(4,128)(2,1)S(1)}, bf16[4,1,18,320]{3,0,2,1:T(4,128)(2,1)S(1)}, u32[]{:S(2)}, u32[]{:S(2)}) collective-permute-start(bf16[4,1,18,320]{3,0,2,1:T(4,128)(2,1)S(1)} %get-tuple-element.17), channel_id=1, source_target_pairs={{1,0},{2,1},{3,2},{5,4},{6,5},{7,6},{9,8},{10,9},{11,10},{13,12},{... | collective-permute-start | bytes 138248 | tf_op jit(solution)/shard_map/ppermute | solution.py:17
  39.0 4.7 %collective-permute-start.3 = (bf16[4,1,18,320]{3,0,2,1:T(4,128)(2,1)S(1)}, bf16[4,1,18,320]{3,0,2,1:T(4,128)(2,1)S(1)}, u32[]{:S(2)}, u32[]{:S(2)}) collective-permute-start(bf16[4,1,18,320]{3,0,2,1:T(4,128)(2,1)S(1)} %get-tuple-element.18), channel_id=1, source_target_pairs={{0,1},{1,2},{2,3},{4,5},{5,6},{6,7},{8,9},{9,10},{10,11},{12,13},{... | collective-permute-start | bytes 138248 | tf_op jit(solution)/shard_map/ppermute | solution.py:16
  43.7 1.6 %collective-permute-start.2 = (bf16[4,18,320]{2,0,1:T(4,128)(2,1)S(1)}, bf16[4,18,320]{2,0,1:T(4,128)(2,1)S(1)}, u32[]{:S(2)}, u32[]{:S(2)}) collective-permute-start(bf16[4,18,320]{2,0,1:T(4,128)(2,1)S(1)} %bitcast.79), channel_id=1, source_target_pairs={{0,16},{4,20},{8,24},{12,28},{16,0},{20,4},{24,8},{28,12},{1,17},{... | collective-permute-start | bytes 138248 | tf_op jit(solution)/shard_map/ppermute | solution.py:24
  45.4 2.6 %collective-permute-done.2 = bf16[4,18,320]{2,0,1:T(4,128)(2,1)S(1)} collective-permute-done((bf16[4,18,320]{2,0,1:T(4,128)(2,1)S(1)}, bf16[4,18,320]{2,0,1:T(4,128)(2,1)S(1)}, u32[]{:S(2)}, u32[]{:S(2)}) %collective-permute-start.2) | collective-permute-done | bytes 46112 | tf_op jit(solution)/shard_map/ppermute | solution.py:24
  48.0 0.9 maximum_bitcast_fusion.1
  48.9 0.5 pad
  49.4 0.3 slice.44
  49.7 1.0 fusion.5
  50.8 0.2 broadcast.25
  51.0 0.5 copy-done.7
  51.5 7.1 %fusion.30 = (f32[16,32,3,320]{3,1,2,0:T(8,128)S(1)}, f32[16,32,3,320]{3,1,2,0:T(8,128)}) fusion(f32[16,32,3,320]{3,0,2,1:T(8,128)S(1)} %bitcast.75, f32[320]{0:T(512)S(1)} %copy-done.7, bf16[3,3,320,320]{3,2,1,0:T(8,128)(2,1)S(1)} %copy-done, bf16[18,4,8,5,320]{4,1,3,2,0:T(4,128)(2,1)S(1)} %fusion.5, pred[32,3]{0,1:T(4,128)(4,1)S(1)} %copy-done.9), kind=kOutput, calls=%fused_computation.59 | convolution fusion | flops 2834104320 | bytes 9586016 | tf_op jit(solution)/shard_map/conv_general_dilated | solution.py:73
  58.5 1.4 %copy.121 = f32[16,32,3,320]{3,0,2,1:T(8,128)S(1)} copy(f32[16,32,3,320]{3,1,2,0:T(8,128)S(1)} %get-tuple-element.27) | data formatting | bytes 3932160 | tf_op jit(solution)/shard_map/mul | solution.py:39
  59.9 0.1 slice_reduce_fusion
  60.0 0.1 reduce_sum.74
  60.1 0.1 reduce_sum.75
  60.2 3.0 %copy.119 = f32[16,32,3,320]{3,0,2,1:T(8,128)S(1)} copy(f32[16,32,3,320]{3,1,2,0:T(8,128)} %get-tuple-element.28) | data formatting | bytes 3932160 | tf_op jit(solution)/shard_map/convert_element_type | solution.py:67
  63.3 0.1 slice_reduce_fusion.1
  63.4 0.1 reduce_sum.59
  63.5 0.1 reduce_sum.72
  63.6 12.5 %all-reduce = (f32[4,32]{1,0:T(4,128)S(1)}, f32[4,32]{1,0:T(4,128)S(1)}) all-reduce(f32[4,32]{1,0:T(4,128)S(1)} %reduce_sum.75, f32[4,32]{1,0:T(4,128)S(1)} %reduce_sum.72), channel_id=1, replica_groups=mesh['lon'=8,'lat'=4] {'lon'}, use_global_device_ids=true, to_apply=%region_14.15 | all-reduce | flops 256 | bytes 2048 | tf_op jit(solution)/shard_map/psum | solution.py:35
  76.0 8.9 %all-reduce.2 = (f32[4,32]{1,0:T(4,128)S(1)}, f32[4,32]{1,0:T(4,128)S(1)}) all-reduce(f32[4,32]{1,0:T(4,128)S(1)} %get-tuple-element.7, f32[4,32]{1,0:T(4,128)S(1)} %get-tuple-element.8), channel_id=1, replica_groups=mesh['lon'=8,'lat'=4] {'lat'}, use_global_device_ids=true, to_apply=%region_15.16 | all-reduce | flops 256 | bytes 2048 | tf_op jit(solution)/shard_map/psum | solution.py:35
  85.0 0.1 sub.30
  85.2 0.1 mul.67
  85.3 0.2 broadcast.27
  85.5 0.2 broadcast.26
  85.7 1.3 %copy-done.1 = f32[16,32,3,320]{3,1,2,0:T(8,128)S(1)} copy-done((f32[16,32,3,320]{3,1,2,0:T(8,128)S(1)}, f32[16,32,3,320]{3,1,2,0:T(8,128)}, u32[]{:S(2)}) %copy-start.1) | copy-done | bytes 1966104
  87.0 1.8 %multiply_convert_fusion = bf16[16,32,3,320]{3,1,2,0:T(8,128)(2,1)S(1)} fusion(f32[16,32,3,320]{3,0,2,1:T(8,128)S(1)} %bitcast.65, f32[16,32,3,320]{3,1,2,0:T(8,128)S(1)} %copy-done.1, f32[16,32,3,320]{3,0,2,1:T(8,128)S(1)} %bitcast.66, f32[320]{0:T(512)S(1)} %copy-done.4, f32[320]{0:T(512)S(1)} %copy-done.5), kind=kLoop, calls=%fused_computation.14 | loop fusion | flops 4423680 | bytes 6883840 | tf_op jit(solution)/shard_map/convert_element_type | solution.py:51
  88.8 0.4 copy.123
  89.4 2.6 %collective-permute-start.7 = (bf16[4,16,1,320]{3,1,2,0:T(8,128)(2,1)S(1)}, bf16[4,16,1,320]{3,1,2,0:T(8,128)(2,1)S(1)}, u32[]{:S(2)}, u32[]{:S(2)}) collective-permute-start(bf16[4,16,1,320]{3,1,2,0:T(8,128)(2,1)S(1)} %get-tuple-element.20), channel_id=1, source_target_pairs={{4,0},{8,4},{12,8},{16,12},{20,16},{24,20},{28,24},{0,28},{5,1},{9... | collective-permute-start | bytes 122888 | tf_op jit(solution)/shard_map/ppermute | solution.py:17
  92.0 1.8 %collective-permute-done.6 = bf16[4,16,1,320]{3,1,2,0:T(8,128)(2,1)S(1)} collective-permute-done((bf16[4,16,1,320]{3,1,2,0:T(8,128)(2,1)S(1)}, bf16[4,16,1,320]{3,1,2,0:T(8,128)(2,1)S(1)}, u32[]{:S(2)}, u32[]{:S(2)}) %collective-permute-start.6) | collective-permute-done | bytes 40992 | tf_op jit(solution)/shard_map/ppermute | solution.py:16
  93.8 0.2 pad_maximum_fusion.2
  94.0 1.6 %collective-permute-start.10 = (bf16[4,18,320]{2,0,1:T(4,128)(2,1)S(1)}, bf16[4,18,320]{2,0,1:T(4,128)(2,1)S(1)}, u32[]{:S(2)}, u32[]{:S(2)}) collective-permute-start(bf16[4,18,320]{2,0,1:T(4,128)(2,1)S(1)} %bitcast.77), channel_id=1, source_target_pairs={{0,16},{4,20},{8,24},{12,28},{16,0},{20,4},{24,8},{28,12},{1,17},{... | collective-permute-start | bytes 138248 | tf_op jit(solution)/shard_map/ppermute | solution.py:24
  95.6 1.3 %collective-permute-start.11 = (bf16[4,1,18,320]{3,1,2,0:T(2,128)(2,1)S(1)}, bf16[4,1,18,320]{3,1,2,0:T(2,128)(2,1)S(1)}, u32[]{:S(2)}, u32[]{:S(2)}) collective-permute-start(bf16[4,1,18,320]{3,1,2,0:T(2,128)(2,1)S(1)} %get-tuple-element.15), channel_id=1, source_target_pairs={{1,0},{2,1},{3,2},{5,4},{6,5},{7,6},{9,8},{10,9},{11,10},{13,12},{... | collective-permute-start | bytes 138248 | tf_op jit(solution)/shard_map/ppermute | solution.py:17
  96.9 4.6 %collective-permute-start.9 = (bf16[4,1,18,320]{3,1,2,0:T(2,128)(2,1)S(1)}, bf16[4,1,18,320]{3,1,2,0:T(2,128)(2,1)S(1)}, u32[]{:S(2)}, u32[]{:S(2)}) collective-permute-start(bf16[4,1,18,320]{3,1,2,0:T(2,128)(2,1)S(1)} %get-tuple-element.16), channel_id=1, source_target_pairs={{0,1},{1,2},{2,3},{4,5},{5,6},{6,7},{8,9},{9,10},{10,11},{12,13},{... | collective-permute-start | bytes 138248 | tf_op jit(solution)/shard_map/ppermute | solution.py:16
  101.5 0.6 collective-permute-start.8
  102.0 0.2 collective-permute-done.11
  102.3 0.1 copy.129
  102.4 3.3 %collective-permute-done.8 = bf16[4,18,320]{2,0,1:T(4,128)(2,1)S(1)} collective-permute-done((bf16[4,18,320]{2,0,1:T(4,128)(2,1)S(1)}, bf16[4,18,320]{2,0,1:T(4,128)(2,1)S(1)}, u32[]{:S(2)}, u32[]{:S(2)}) %collective-permute-start.8) | collective-permute-done | bytes 46112 | tf_op jit(solution)/shard_map/ppermute | solution.py:24
  105.8 0.9 maximum_bitcast_fusion
  106.7 0.4 copy.136
  107.1 0.5 pad.2.clone
  107.6 0.3 slice.50
  107.9 1.0 fusion.6
  109.0 0.5 copy-done.6
  109.5 5.0 %select_add_fusion = f32[16,32,3,320]{3,1,2,0:T(8,128)S(1)} fusion(bf16[3,3,320,320]{3,2,1,0:T(8,128)(2,1)S(1)} %copy-done.6, bf16[18,4,8,5,320]{4,1,3,2,0:T(4,128)(2,1)S(1)} %fusion.6, f32[320]{0:T(512)S(1)} %copy-done.8, pred[32,3]{0,1:T(4,128)(4,1)S(1)} %copy-done.9), kind=kOutput, calls=%fused_computation.13 | convolution fusion | flops 2832138240 | bytes 5653856 | tf_op jit(solution)/shard_map/conv_general_dilated | solution.py:73
  114.5 1.4 %copy.132 = f32[16,32,3,320]{3,0,2,1:T(8,128)S(1)} copy(f32[16,32,3,320]{3,1,2,0:T(8,128)S(1)} %select_add_fusion) | data formatting | bytes 3932160 | tf_op jit(solution)/shard_map/add | solution.py:103
  115.9 0.1 slice.51
  116.0 1.0 copy-done.2
  117.0 1.4 %fusion.17 = bf16[4,16,16,320]{3,0,2,1:T(4,128)(2,1)S(1)} fusion(f32[16,4,16,320]{3,0,2,1:T(8,128)S(1)} %slice.51, bf16[4,16,16,320]{3,2,1,0:T(8,128)(2,1)S(1)} %copy-done.2), kind=kLoop, calls=%fused_computation.28 | loop fusion | flops 983040 | bytes 2621440 | tf_op jit(solution)/shard_map/convert_element_type | solution.py:104
  118.5 1.0 copy.134
  (41 shorter events, 0.9 us)
Async XLA Ops:
  0.0 51.0 %copy-start = (bf16[3,3,320,320]{3,2,1,0:T(8,128)(2,1)S(1)}, bf16[3,3,320,320]{3,2,1,0:T(8,128)(2,1)}, u32[]{:S(2)}) copy-start(bf16[3,3,320,320]{3,2,1,0:T(8,128)(2,1)} %param.13) | copy-start | bytes 5529604
  32.6 4.5 %collective-permute-start = (bf16[4,16,1,320]{3,0,2,1:T(4,128)(2,1)S(1)}, bf16[4,16,1,320]{3,0,2,1:T(4,128)(2,1)S(1)}, u32[]{:S(2)}, u32[]{:S(2)}) collective-permute-start(bf16[4,16,1,320]{3,0,2,1:T(4,128)(2,1)S(1)} %get-tuple-element.21), channel_id=1, source_target_pairs={{0,4},{4,8},{8,12},{12,16},{16,20},{20,24},{24,28},{28,0},{1,5},{5... | collective-permute-start | bytes 122888 | tf_op jit(solution)/shard_map/ppermute | solution.py:16
  32.6 4.4 %collective-permute-start.1 = (bf16[4,16,1,320]{3,0,2,1:T(4,128)(2,1)S(1)}, bf16[4,16,1,320]{3,0,2,1:T(4,128)(2,1)S(1)}, u32[]{:S(2)}, u32[]{:S(2)}) collective-permute-start(bf16[4,16,1,320]{3,0,2,1:T(4,128)(2,1)S(1)} %get-tuple-element.22), channel_id=1, source_target_pairs={{4,0},{8,4},{12,8},{16,12},{20,16},{24,20},{28,24},{0,28},{5,1},{9... | collective-permute-start | bytes 122888 | tf_op jit(solution)/shard_map/ppermute | solution.py:17
  37.1 8.2 %collective-permute-start.4 = (bf16[4,18,320]{2,0,1:T(4,128)(2,1)S(1)}, bf16[4,18,320]{2,0,1:T(4,128)(2,1)S(1)}, u32[]{:S(2)}, u32[]{:S(2)}) collective-permute-start(bf16[4,18,320]{2,0,1:T(4,128)(2,1)S(1)} %bitcast.78), channel_id=1, source_target_pairs={{0,16},{4,20},{8,24},{12,28},{16,0},{20,4},{24,8},{28,12},{1,17},{... | collective-permute-start | bytes 138248 | tf_op jit(solution)/shard_map/ppermute | solution.py:24
  37.7 7.6 %collective-permute-start.5 = (bf16[4,1,18,320]{3,0,2,1:T(4,128)(2,1)S(1)}, bf16[4,1,18,320]{3,0,2,1:T(4,128)(2,1)S(1)}, u32[]{:S(2)}, u32[]{:S(2)}) collective-permute-start(bf16[4,1,18,320]{3,0,2,1:T(4,128)(2,1)S(1)} %get-tuple-element.17), channel_id=1, source_target_pairs={{1,0},{2,1},{3,2},{5,4},{6,5},{7,6},{9,8},{10,9},{11,10},{13,12},{... | collective-permute-start | bytes 138248 | tf_op jit(solution)/shard_map/ppermute | solution.py:17
  39.0 9.0 %collective-permute-start.3 = (bf16[4,1,18,320]{3,0,2,1:T(4,128)(2,1)S(1)}, bf16[4,1,18,320]{3,0,2,1:T(4,128)(2,1)S(1)}, u32[]{:S(2)}, u32[]{:S(2)}) collective-permute-start(bf16[4,1,18,320]{3,0,2,1:T(4,128)(2,1)S(1)} %get-tuple-element.18), channel_id=1, source_target_pairs={{0,1},{1,2},{2,3},{4,5},{5,6},{6,7},{8,9},{9,10},{10,11},{12,13},{... | collective-permute-start | bytes 138248 | tf_op jit(solution)/shard_map/ppermute | solution.py:16
  43.7 4.2 %collective-permute-start.2 = (bf16[4,18,320]{2,0,1:T(4,128)(2,1)S(1)}, bf16[4,18,320]{2,0,1:T(4,128)(2,1)S(1)}, u32[]{:S(2)}, u32[]{:S(2)}) collective-permute-start(bf16[4,18,320]{2,0,1:T(4,128)(2,1)S(1)} %bitcast.79), channel_id=1, source_target_pairs={{0,16},{4,20},{8,24},{12,28},{16,0},{20,4},{24,8},{28,12},{1,17},{... | collective-permute-start | bytes 138248 | tf_op jit(solution)/shard_map/ppermute | solution.py:24
  49.7 1.1 copy-start.3
  50.8 0.7 copy-start.7
  50.8 0.7 copy-start.9
  85.3 1.7 %copy-start.1 = (f32[16,32,3,320]{3,1,2,0:T(8,128)S(1)}, f32[16,32,3,320]{3,1,2,0:T(8,128)}, u32[]{:S(2)}) copy-start(f32[16,32,3,320]{3,1,2,0:T(8,128)} %get-tuple-element.28) | copy-start | bytes 5898244
  85.3 1.7 %copy-start.4 = (f32[320]{0:T(512)S(1)}, f32[320]{0:T(512)}, u32[]{:S(2)}) copy-start(f32[320]{0:T(512)} %param.17) | copy-start | bytes 3844
  85.3 1.7 %copy-start.5 = (f32[320]{0:T(512)S(1)}, f32[320]{0:T(512)}, u32[]{:S(2)}) copy-start(f32[320]{0:T(512)} %param.16) | copy-start | bytes 3844
  89.3 4.5 %collective-permute-start.6 = (bf16[4,16,1,320]{3,1,2,0:T(8,128)(2,1)S(1)}, bf16[4,16,1,320]{3,1,2,0:T(8,128)(2,1)S(1)}, u32[]{:S(2)}, u32[]{:S(2)}) collective-permute-start(bf16[4,16,1,320]{3,1,2,0:T(8,128)(2,1)S(1)} %get-tuple-element.19), channel_id=1, source_target_pairs={{0,4},{4,8},{8,12},{12,16},{16,20},{20,24},{24,28},{28,0},{1,5},{5... | collective-permute-start | bytes 122888 | tf_op jit(solution)/shard_map/ppermute | solution.py:16
  89.4 4.4 %collective-permute-start.7 = (bf16[4,16,1,320]{3,1,2,0:T(8,128)(2,1)S(1)}, bf16[4,16,1,320]{3,1,2,0:T(8,128)(2,1)S(1)}, u32[]{:S(2)}, u32[]{:S(2)}) collective-permute-start(bf16[4,16,1,320]{3,1,2,0:T(8,128)(2,1)S(1)} %get-tuple-element.20), channel_id=1, source_target_pairs={{4,0},{8,4},{12,8},{16,12},{20,16},{24,20},{28,24},{0,28},{5,1},{9... | collective-permute-start | bytes 122888 | tf_op jit(solution)/shard_map/ppermute | solution.py:17
  94.0 8.0 %collective-permute-start.10 = (bf16[4,18,320]{2,0,1:T(4,128)(2,1)S(1)}, bf16[4,18,320]{2,0,1:T(4,128)(2,1)S(1)}, u32[]{:S(2)}, u32[]{:S(2)}) collective-permute-start(bf16[4,18,320]{2,0,1:T(4,128)(2,1)S(1)} %bitcast.77), channel_id=1, source_target_pairs={{0,16},{4,20},{8,24},{12,28},{16,0},{20,4},{24,8},{28,12},{1,17},{... | collective-permute-start | bytes 138248 | tf_op jit(solution)/shard_map/ppermute | solution.py:24
  95.6 6.6 %collective-permute-start.11 = (bf16[4,1,18,320]{3,1,2,0:T(2,128)(2,1)S(1)}, bf16[4,1,18,320]{3,1,2,0:T(2,128)(2,1)S(1)}, u32[]{:S(2)}, u32[]{:S(2)}) collective-permute-start(bf16[4,1,18,320]{3,1,2,0:T(2,128)(2,1)S(1)} %get-tuple-element.15), channel_id=1, source_target_pairs={{1,0},{2,1},{3,2},{5,4},{6,5},{7,6},{9,8},{10,9},{11,10},{13,12},{... | collective-permute-start | bytes 138248 | tf_op jit(solution)/shard_map/ppermute | solution.py:17
  96.9 8.8 %collective-permute-start.9 = (bf16[4,1,18,320]{3,1,2,0:T(2,128)(2,1)S(1)}, bf16[4,1,18,320]{3,1,2,0:T(2,128)(2,1)S(1)}, u32[]{:S(2)}, u32[]{:S(2)}) collective-permute-start(bf16[4,1,18,320]{3,1,2,0:T(2,128)(2,1)S(1)} %get-tuple-element.16), channel_id=1, source_target_pairs={{0,1},{1,2},{2,3},{4,5},{5,6},{6,7},{8,9},{9,10},{10,11},{12,13},{... | collective-permute-start | bytes 138248 | tf_op jit(solution)/shard_map/ppermute | solution.py:16
  101.5 4.2 %collective-permute-start.8 = (bf16[4,18,320]{2,0,1:T(4,128)(2,1)S(1)}, bf16[4,18,320]{2,0,1:T(4,128)(2,1)S(1)}, u32[]{:S(2)}, u32[]{:S(2)}) collective-permute-start(bf16[4,18,320]{2,0,1:T(4,128)(2,1)S(1)} %bitcast.76), channel_id=1, source_target_pairs={{0,16},{4,20},{8,24},{12,28},{16,0},{20,4},{24,8},{28,12},{1,17},{... | collective-permute-start | bytes 138248 | tf_op jit(solution)/shard_map/ppermute | solution.py:24
  107.9 1.6 %copy-start.6 = (bf16[3,3,320,320]{3,2,1,0:T(8,128)(2,1)S(1)}, bf16[3,3,320,320]{3,2,1,0:T(8,128)(2,1)}, u32[]{:S(2)}) copy-start(bf16[3,3,320,320]{3,2,1,0:T(8,128)(2,1)} %param.18) | copy-start | bytes 5529604
  107.9 1.6 %copy-start.8 = (f32[320]{0:T(512)S(1)}, f32[320]{0:T(512)}, u32[]{:S(2)}) copy-start(f32[320]{0:T(512)} %param.19) | copy-start | bytes 3844
  115.9 1.1 copy-start.2
